TPU v7x, 128 devices: a whole 4x4x4 slice. The times are simulated.
128 devices in a mesh: row: 8 (over x_hi, y), col: 16 (over z, x_lo, core).
Axes of the slice: x: 4 (x_hi: 2, x_lo: 2; x = x_hi * 2 + x_lo), y: 4, z: 4, core: 2. Of those that a mesh axis runs over, the one named last changes fastest.
Arguments:
- fields: bfloat16 [128, 128, 1024], P('row', 'col'), may hold values from -6 to 6
- cotangent: bfloat16 [128, 128, 1024], P('row', 'col'), may hold values from -6 to 6
- query_weight: bfloat16 [1024, 1024], P(('row', 'col')), may hold values from -1 to 6
- key_weight: bfloat16 [1024, 1024], P(('row', 'col')), may hold values from -1 to 6
- value_weight: bfloat16 [1024, 1024], P(('row', 'col')), may hold values from -0.1875 to 0.1875
- output_weight: bfloat16 [1024, 1024], P(('row', 'col')), may hold values from -0.1875 to 0.1875
- expert_ids: int32 [8, 16, 128, 2], P('row', 'col'), may hold values from 0 to 31, all different within a row; in each aligned block of 128 rows (0 to 127, 128 to 255, ..., all dimensions but the last counted through in order) at most 10 rows name the same one
- gate_values: float32 [8, 16, 128, 2], P('row', 'col'), may hold values from 0.2 to 1
- gate_weight: bfloat16 [128, 1024, 1024], P(('row', 'col')), may hold values from -0.1875 to 0.1875
- up_weight: bfloat16 [128, 1024, 1024], P(('row', 'col')), may hold values from -0.1875 to 0.1875
- down_weight: bfloat16 [128, 1024, 1024], P(('row', 'col')), may hold values from -0.09375 to 0.09375
Outputs:
- field_grad: bfloat16 [128, 128, 1024], P('row', 'col')
- gate_grad: bfloat16 [128, 1024, 1024], P(('row', 'col'))
- up_grad: bfloat16 [128, 1024, 1024], P(('row', 'col'))
- down_grad: bfloat16 [128, 1024, 1024], P(('row', 'col'))
Inputs may be any that keep to these rules, and one draw needn't show every extreme that they name: `expert_ids`: the 2 entries of a cell differ; among one device's 128 cells no expert is named more than 10 times, a bound that some block reaches.
All inputs are finite; a program needn't handle non-finite values.
Results may differ from a plain program's by a relative error of at most 0.0095.
Values may be sent and summed in bfloat16 or wider, within the bound.
No kernel may reach another device: no remote copies, remote signals or barrier semaphores. Data moves between devices by JAX's collectives and lax.ppermute only.
A program may use at most 192 MiB of HBM per device.

v0:
```python
import math
import jax
import jax.numpy as jnp
from jax import lax
from jax.sharding import PartitionSpec as P

HEADS = 16
EXPERTS = 32
CAP = 10
EPS = 1e-06


def normalize(values):
    scale = lax.rsqrt(jnp.mean(values * values, axis=-1, keepdims=True) + EPS)
    return (values * scale, scale)


def norm_back(grads, normed, scale):
    return scale * (grads - normed * jnp.mean(grads * normed, axis=-1, keepdims=True))


def contract_rows(left, right):
    return lax.dot_general(
        left, right, (((0,), (0,)), ((), ())), preferred_element_type=jnp.float32
    )


def times_transposed(left, right):
    return lax.dot_general(
        left, right, (((1,), (1,)), ((), ())), preferred_element_type=jnp.float32
    )


def attention_forward(normed_half, query_weight, key_weight, value_weight, output_weight):
    latitudes, longitudes, features = normed_half.shape
    head_size = features // HEADS
    flat_rows = normed_half.reshape(latitudes * longitudes, features)

    def project(weight):
        result = jnp.dot(flat_rows, weight, preferred_element_type=jnp.float32)
        return result.astype(jnp.bfloat16).reshape(latitudes, longitudes, HEADS, head_size)

    queries = project(query_weight)
    key_rows = project(key_weight)
    value_rows = project(value_weight)
    factor = 1.0 / math.sqrt(head_size)
    scores = (
        jnp.einsum("bqhd,bkhd->bhqk", queries, key_rows, preferred_element_type=jnp.float32)
        * factor
    )
    attention = jax.nn.softmax(scores, axis=-1)
    attention_half = attention.astype(jnp.bfloat16)
    attended = jnp.einsum(
        "bhqk,bkhd->bqhd", attention_half, value_rows, preferred_element_type=jnp.float32
    ).astype(jnp.bfloat16)
    mixture = jnp.dot(
        attended.reshape(latitudes * longitudes, features),
        output_weight,
        preferred_element_type=jnp.float32,
    )
    return (mixture, (queries, key_rows, value_rows, attention, attention_half))


def attention_backward(block_half, stored, query_weight, key_weight, value_weight, output_weight):
    queries, key_rows, value_rows, attention, attention_half = stored
    latitudes, longitudes, head_count, head_size = queries.shape
    features = head_count * head_size
    factor = 1.0 / math.sqrt(head_size)
    out_grad = times_transposed(block_half.reshape(-1, features), output_weight)
    out_grad = out_grad.astype(jnp.bfloat16).reshape(latitudes, longitudes, head_count, head_size)
    mass_grad = jnp.einsum(
        "bqhd,bkhd->bhqk", out_grad, value_rows, preferred_element_type=jnp.float32
    )
    score_grad = (
        attention * (mass_grad - jnp.sum(attention * mass_grad, axis=-1, keepdims=True)) * factor
    )
    score_grad = score_grad.astype(jnp.bfloat16)
    query_grad = jnp.einsum(
        "bhqk,bkhd->bqhd", score_grad, key_rows, preferred_element_type=jnp.float32
    ).astype(jnp.bfloat16)
    key_grad = jnp.einsum(
        "bhqk,bqhd->bkhd", score_grad, queries, preferred_element_type=jnp.float32
    ).astype(jnp.bfloat16)
    value_grad = jnp.einsum(
        "bhqk,bqhd->bkhd", attention_half, out_grad, preferred_element_type=jnp.float32
    ).astype(jnp.bfloat16)
    total = times_transposed(query_grad.reshape(-1, features), query_weight)
    total = total + times_transposed(key_grad.reshape(-1, features), key_weight)
    return total + times_transposed(value_grad.reshape(-1, features), value_weight)


def expert_terms(inputs, mix_grad, gate_block, up_block, down_block):
    gate_pre = jnp.dot(inputs, gate_block, preferred_element_type=jnp.float32)
    up_pre = jnp.dot(inputs, up_block, preferred_element_type=jnp.float32)
    sigmoid_gate = jax.nn.sigmoid(gate_pre)
    swish_gate = gate_pre * sigmoid_gate
    hidden = (swish_gate * up_pre).astype(jnp.bfloat16)
    hidden_grad = times_transposed(mix_grad, down_block)
    gate_delta = (
        hidden_grad * up_pre * sigmoid_gate * (1.0 + gate_pre * (1.0 - sigmoid_gate))
    ).astype(jnp.bfloat16)
    up_delta = (hidden_grad * swish_gate).astype(jnp.bfloat16)
    down_term = contract_rows(hidden, mix_grad).astype(jnp.bfloat16)
    gate_term = contract_rows(inputs, gate_delta).astype(jnp.bfloat16)
    up_term = contract_rows(inputs, up_delta).astype(jnp.bfloat16)
    returned = times_transposed(gate_delta, gate_block) + times_transposed(up_delta, up_block)
    return (gate_term, up_term, down_term, returned)


def assignment_slots(chosen):
    onehot = (chosen[:, None] == jnp.arange(EXPERTS, dtype=jnp.int32)[None, :]).astype(jnp.int32)
    before = jnp.cumsum(onehot, axis=0) - onehot
    return jnp.sum(before * onehot, axis=1)


def body(
    fields,
    cotangent,
    query_weight,
    key_weight,
    value_weight,
    output_weight,
    expert_ids,
    gate_values,
    gate_weight,
    up_weight,
    down_weight,
):
    field_rows, cotangent_rows = (
        lax.all_to_all(fields, "col", split_axis=0, concat_axis=1, tiled=True),
        lax.all_to_all(cotangent, "col", split_axis=0, concat_axis=1, tiled=True),
    )
    query_all, key_all, value_all, output_all = (
        lax.all_gather(query_weight, ("row", "col"), axis=0, tiled=True),
        lax.all_gather(key_weight, ("row", "col"), axis=0, tiled=True),
        lax.all_gather(value_weight, ("row", "col"), axis=0, tiled=True),
        lax.all_gather(output_weight, ("row", "col"), axis=0, tiled=True),
    )
    latitudes, longitudes, features = field_rows.shape
    token_count = latitudes * longitudes
    top_count = expert_ids.shape[-1]
    fields_full = field_rows.astype(jnp.float32)
    normed_in, scale_in = normalize(fields_full)
    normed_in_half = normed_in.astype(jnp.bfloat16)
    mixture, stored = attention_forward(normed_in_half, query_all, key_all, value_all, output_all)
    mid_stream = (fields_full.reshape(token_count, features) + mixture).astype(jnp.bfloat16)
    normed_mid, scale_mid = normalize(mid_stream.astype(jnp.float32))
    normed_mid_half = normed_mid.astype(jnp.bfloat16)
    chosen = expert_ids.reshape(token_count * top_count)
    slot_index = assignment_slots(chosen)
    places = chosen * CAP + slot_index
    cotangent_full = cotangent_rows.reshape(token_count, features).astype(jnp.float32)
    weights = gate_values.reshape(token_count, top_count)
    mix_grad = (
        (weights[:, :, None] * cotangent_full[:, None, :])
        .astype(jnp.bfloat16)
        .reshape(token_count * top_count, features)
    )
    inputs = jnp.broadcast_to(
        normed_mid_half[:, None, :], (token_count, top_count, features)
    ).reshape(token_count * top_count, features)
    blank_buffer = jnp.zeros((EXPERTS * CAP, features), jnp.bfloat16)
    send_inputs = blank_buffer.at[places].set(inputs)
    send_grads = blank_buffer.at[places].set(mix_grad)
    row_devices = lax.axis_size("row")
    col_devices = lax.axis_size("col")
    all_devices = row_devices * col_devices
    slice_count = all_devices // EXPERTS

    def spread(buffer):
        widened = jnp.broadcast_to(
            buffer.reshape(EXPERTS, 1, CAP, features), (EXPERTS, slice_count, CAP, features)
        )
        return widened.reshape(all_devices, CAP, features)

    recv_inputs, recv_grads = (
        lax.all_to_all(
            spread(send_inputs), ("row", "col"), split_axis=0, concat_axis=0, tiled=True
        ),
        lax.all_to_all(spread(send_grads), ("row", "col"), split_axis=0, concat_axis=0, tiled=True),
    )
    row_count = all_devices * CAP
    gate_term, up_term, down_term, returned = expert_terms(
        recv_inputs.reshape(row_count, features),
        recv_grads.reshape(row_count, features),
        gate_weight[0],
        up_weight[0],
        down_weight[0],
    )
    coming_back = lax.all_to_all(
        returned.reshape(all_devices, CAP, features).astype(jnp.bfloat16),
        ("row", "col"),
        split_axis=0,
        concat_axis=0,
        tiled=True,
    ).astype(jnp.float32)
    summed = jnp.sum(coming_back.reshape(EXPERTS, slice_count, CAP, features), axis=1)
    gathered = summed.reshape(EXPERTS * CAP, features)[places]
    normed_grad = jnp.sum(gathered.reshape(token_count, top_count, features), axis=1)
    block_grad = cotangent_full + norm_back(normed_grad, normed_mid, scale_mid)
    block_half = block_grad.astype(jnp.bfloat16)
    branch_grad = attention_backward(
        block_half.reshape(latitudes, longitudes, features),
        stored,
        query_all,
        key_all,
        value_all,
        output_all,
    )
    field_total = block_grad + norm_back(
        branch_grad, normed_in.reshape(token_count, features), scale_in.reshape(token_count, 1)
    )
    field_half = field_total.astype(jnp.bfloat16).reshape(latitudes, longitudes, features)
    field_grad = lax.all_to_all(field_half, "col", split_axis=1, concat_axis=0, tiled=True)
    return (field_grad, gate_term[None], up_term[None], down_term[None])


def solution(mesh):
    in_specs = (
        P("row", "col", None),
        P("row", "col", None),
        P(("row", "col"), None),
        P(("row", "col"), None),
        P(("row", "col"), None),
        P(("row", "col"), None),
        P("row", "col", None, None),
        P("row", "col", None, None),
        P(("row", "col"), None, None),
        P(("row", "col"), None, None),
        P(("row", "col"), None, None),
    )
    out_specs = (
        P("row", "col", None),
        P(("row", "col"), None, None),
        P(("row", "col"), None, None),
        P(("row", "col"), None, None),
    )
    return jax.shard_map(body, mesh=mesh, in_specs=in_specs, out_specs=out_specs, check_vma=False)
```

profile of v0, /device:TPU:1, one launch (start us, length us, event | category | flops | bytes accessed | tf_op | source)
XLA Modules:
  0.0 1054.5 jit_solution(7280352464968909564)
XLA Ops:
  10.0 7.8 all-to-all-start
  20.7 4.3 all-to-all-done
  24.9 4.2 all-to-all-start.1
  30.2 1.3 mul.151
  31.5 1.9 mul.152
  33.5 2.6 scatter_custom_fusion
  36.0 1.3 broadcast_in_dim.19
  37.3 2.5 broadcast_in_dim.20
  39.8 9.7 all-to-all-start.2
  49.8 195.3 %all-gather.7.cloned.1.call-done = bf16[1024,1024]{1,0:T(8,128)(2,1)} async-done(((bf16[8,1024]{1,0:T(8,128)(2,1)}), bf16[1024,1024]{1,0:T(8,128)(2,1)}) %all-gather.7.cloned.1.call-update) | async-done | bytes 2097168 | tf_op jit(solution)/shard_map/all_gather | solution.py:134
  245.1 2.1 convolution_convert_fusion.6
  247.4 193.8 %all-gather.9.cloned.1.call-done = bf16[1024,1024]{1,0:T(8,128)(2,1)} async-done(((bf16[8,1024]{1,0:T(8,128)(2,1)}), bf16[1024,1024]{1,0:T(8,128)(2,1)}) %all-gather.9.cloned.1.call-update) | async-done | bytes 2097168 | tf_op jit(solution)/shard_map/all_gather | solution.py:135
  441.2 2.1 convolution_convert_fusion.5
  443.4 193.8 %all-gather.5.cloned.1.call-done = bf16[1024,1024]{1,0:T(8,128)(2,1)} async-done(((bf16[8,1024]{1,0:T(8,128)(2,1)}), bf16[1024,1024]{1,0:T(8,128)(2,1)}) %all-gather.5.cloned.1.call-update) | async-done | bytes 2097168 | tf_op jit(solution)/shard_map/all_gather | solution.py:136
  637.2 2.1 convolution_convert_fusion.7
  639.5 1.5 fusion.61
  641.0 1.4 convolution_convert_fusion.4
  642.4 190.7 %all-gather.11.cloned.1.call-done = bf16[1024,1024]{1,0:T(8,128)(2,1)} async-done(((bf16[8,1024]{1,0:T(8,128)(2,1)}), bf16[1024,1024]{1,0:T(8,128)(2,1)}) %all-gather.11.cloned.1.call-update) | async-done | bytes 2097168 | tf_op jit(solution)/shard_map/all_gather | solution.py:137
  833.1 2.2 multiply_reduce_fusion.2
  836.8 2.4 scatter_custom_fusion.1
  840.3 3.7 broadcast_in_dim.23
  844.0 8.2 all-to-all-start.3
  852.3 6.2 reshape.285
  858.5 46.5 %all-to-all-done.3 = bf16[128,10,1024]{2,1,0:T(8,128)(2,1)} async-done(((bf16[128,10,1024]{2,1,0:T(8,128)(2,1)}), bf16[128,10,1024]{2,1,0:T(8,128)(2,1)}, u32[]{:S(2)}, u32[]{:S(2)}) %all-to-all-start.3) | async-done | bytes 2621472 | tf_op jit(solution)/shard_map/all_to_all | solution.py:177
  905.0 6.1 reshape.288
  911.1 5.4 fusion.6
  916.6 2.9 fusion.9
  920.2 5.9 multiply_convert_fusion.1
  926.1 2.9 fusion.4
  929.1 4.4 add_convert_fusion
  933.4 6.0 convert_element_type.163
  939.4 6.7 all-to-all-start.4
  946.1 6.9 convert_bitcast_fusion.1
  953.1 8.6 convert_bitcast_fusion
  961.6 37.4 %all-to-all-done.4 = bf16[128,10,1024]{2,1,0:T(8,128)(2,1)} async-done(((bf16[128,10,1024]{2,1,0:T(8,128)(2,1)}), bf16[128,10,1024]{2,1,0:T(8,128)(2,1)}, u32[]{:S(2)}, u32[]{:S(2)}) %all-to-all-start.4) | async-done | bytes 2621472 | tf_op jit(solution)/shard_map/all_to_all | solution.py:190
  999.0 4.7 convert_reduce_fusion
  1003.8 1.8 reshape.291
  1005.6 2.0 gather_fusion
  1007.6 3.0 reshape.292
  1010.6 2.5 reduce_sum.89
  1013.3 2.5 convolution_convert_fusion.3
  1017.0 2.6 convolution_convert_fusion
  1020.9 2.7 convolution_convert_fusion.2
  1023.6 3.6 convolution_convert_fusion.1
  1027.2 1.9 fusion.63
  1032.2 2.1 reduce.12
  1035.2 4.3 all-to-all-start.5
  1039.5 6.9 convert_bitcast_fusion.2
  (106 shorter events, 18.4 us)
Async XLA Ops:
  7.2 912.3 %copy-start = (bf16[1,1024,1024]{2,1,0:T(8,128)(2,1)S(1)}, bf16[1,1024,1024]{2,1,0:T(8,128)(2,1)}, u32[]{:S(2)}) copy-start(bf16[1,1024,1024]{2,1,0:T(8,128)(2,1)} %param.21) | copy-start | bytes 6291460
  7.2 237.9 %all-gather.7.cloned.1.call-start = ((), (), s32[]{:S(2)}) async-start(), calls=%async_computation.7 | async-start | bytes 2113536 | tf_op jit(solution)/shard_map/all_gather | solution.py:134
  7.9 433.3 %all-gather.9.cloned.1.call-start = ((), (), s32[]{:S(2)}) async-start(), calls=%async_computation.8 | async-start | bytes 2113536 | tf_op jit(solution)/shard_map/all_gather | solution.py:135
  8.7 628.6 %all-gather.5.cloned.1.call-start = ((), (), s32[]{:S(2)}) async-start(), calls=%async_computation.6 | async-start | bytes 2113536 | tf_op jit(solution)/shard_map/all_gather | solution.py:136
  9.4 823.7 %all-gather.11.cloned.1.call-start = ((), (), s32[]{:S(2)}) async-start(), calls=%async_computation.9 | async-start | bytes 2113536 | tf_op jit(solution)/shard_map/all_gather | solution.py:137
  10.0 15.0 %all-to-all-start = ((bf16[16,8,1024]{2,1,0:T(8,128)(2,1)}), bf16[16,8,1024]{2,1,0:T(8,128)(2,1)S(1)}, u32[]{:S(2)}, u32[]{:S(2)}) async-start(bf16[16,8,1024]{2,1,0:T(8,128)(2,1)} %param.12), calls=%async_computation | async-start | bytes 524288 | tf_op jit(solution)/shard_map/all_to_all | solution.py:131
  24.9 5.2 copy-start.6
  24.9 12.4 %all-to-all-start.1 = ((bf16[16,8,1024]{2,1,0:T(8,128)(2,1)}), bf16[16,8,1024]{2,1,0:T(8,128)(2,1)S(1)}, u32[]{:S(2)}, u32[]{:S(2)}) async-start(bf16[16,8,1024]{2,1,0:T(8,128)(2,1)} %param.11), calls=%async_computation.1 | async-start | bytes 524288 | tf_op jit(solution)/shard_map/all_to_all | solution.py:130
  39.8 800.5 %all-to-all-start.2 = ((bf16[128,10,1024]{2,1,0:T(8,128)(2,1)}), bf16[128,10,1024]{2,1,0:T(8,128)(2,1)}, u32[]{:S(2)}, u32[]{:S(2)}) async-start(bf16[128,10,1024]{2,1,0:T(8,128)(2,1)} %bitcast.161), calls=%async_computation.2 | async-start | bytes 8388608 | tf_op jit(solution)/shard_map/all_to_all | solution.py:180
  247.4 393.6 %copy-start.14 = (bf16[128,1024]{0,1:T(8,128)(2,1)}, bf16[128,1024]{0,1:T(8,128)(2,1)S(1)}, u32[]{:S(2)}) copy-start(bf16[128,1024]{0,1:T(8,128)(2,1)S(1)} %copy.55) | copy-start | bytes 786436
  443.4 198.9 %copy-start.15 = (bf16[128,1024]{0,1:T(8,128)(2,1)}, bf16[128,1024]{0,1:T(8,128)(2,1)S(1)}, u32[]{:S(2)}) copy-start(bf16[128,1024]{0,1:T(8,128)(2,1)S(1)} %copy.56) | copy-start | bytes 786436
  639.5 2.9 copy-start.12
  641.0 1.4 copy-start.21
  844.0 60.9 %all-to-all-start.3 = ((bf16[128,10,1024]{2,1,0:T(8,128)(2,1)}), bf16[128,10,1024]{2,1,0:T(8,128)(2,1)}, u32[]{:S(2)}, u32[]{:S(2)}) async-start(bf16[128,10,1024]{2,1,0:T(8,128)(2,1)} %bitcast.162), calls=%async_computation.3 | async-start | bytes 8388608 | tf_op jit(solution)/shard_map/all_to_all | solution.py:177
  911.1 5.4 copy-start.8
  911.1 5.4 copy-start.20
  916.5 2.9 copy-start.23
  916.6 3.6 copy-start.9
  920.2 5.9 copy-start.24
  920.2 5.9 copy-start.19
  926.1 2.9 copy-start.25
  926.1 3.0 copy-start.26
  939.4 59.6 %all-to-all-start.4 = ((bf16[128,10,1024]{2,1,0:T(8,128)(2,1)}), bf16[128,10,1024]{2,1,0:T(8,128)(2,1)}, u32[]{:S(2)}, u32[]{:S(2)}) async-start(bf16[128,10,1024]{2,1,0:T(8,128)(2,1)} %convert_element_type.163), calls=%async_computation.4 | async-start | bytes 8388608 | tf_op jit(solution)/shard_map/all_to_all | solution.py:190
  946.1 6.9 copy-start.10
  1007.6 5.7 copy-start.5
  1013.1 3.8 copy-start.22
  1016.9 2.6 copy-start.13
  1017.0 3.9 copy-start.16
  1019.9 1.0 copy-start.11
  1023.6 3.6 copy-start.2
  1027.2 2.0 copy-start.3
  1027.2 2.0 copy-start.18
  1027.2 2.8 copy-start.4
  1027.2 2.8 copy-start.17
  1030.0 1.0 copy-start.7
  1035.2 11.4 %all-to-all-start.5 = ((bf16[16,2,4096]{2,1,0:T(2,128)(2,1)}), bf16[16,2,4096]{2,1,0:T(2,128)(2,1)S(1)}, u32[]{:S(2)}, u32[]{:S(2)}) async-start(bf16[16,2,4096]{2,1,0:T(2,128)(2,1)} %reshape.331), calls=%async_computation.5 | async-start | bytes 524288 | tf_op jit(solution)/shard_map/all_to_all | solution.py:214
  1039.5 8.2 copy-start.1
Sparse Core Ops, SparseCore 0:
  9.7 235.3 all-gather.6
  246.8 194.2 all-gather.8
  442.9 194.2 all-gather.4
  638.8 194.2 all-gather.10
where the time goes:
time: 1060 us; the launch traced here: 1050 us
  waiting for transfers between devices  865 us (82%)
  matrix products  70.7 us (7%)
  local copies, waits for them, and re-layouts  49.5 us (5%)
  starting transfers between devices  41.1 us (4%)
  between operations  14.6 us (1%)
  other arithmetic  14.2 us (1%)
    all_gather x1, waiting for transfers between devices, body(): lax.all_gather(query_weight, ('row', 'col'), axis=0, tiled=True)  195 us
    all_gather x1, waiting for transfers between devices, body(): lax.all_gather(key_weight, ('row', 'col'), axis=0, tiled=True)  194 us
    all_gather x1, waiting for transfers between devices, body(): lax.all_gather(value_weight, ('row', 'col'), axis=0, tiled=True)  194 us
    all_gather x1, waiting for transfers between devices, body(): lax.all_gather(output_weight, ('row', 'col'), axis=0, tiled=True)  191 us
    all_to_all x1, waiting for transfers between devices, body(): lax.all_to_all(spread(send_inputs), ('row', 'col'), split_axis=0, concat_...  46.5 us
    all_to_all x1, waiting for transfers between devices, body(): lax.all_to_all(returned.reshape(all_devices, CAP, features).astype(jnp.bf...  37.4 us
    dot_general x3, matrix products, contract_rows(): lax.dot_general(left, right, (((0,), (0,)), ((), ())), preferred_element_...  22.5 us
  transfers between devices with their start and end apart: 10, of which 8 were waited for; matrix products, arithmetic and copies ran while one was open for 6% of the time, Pallas kernels for 0%

commit v1 on v0

--- a/solution.py
+++ b/solution.py
@@ -133,7 +133,12 @@
     query_all, key_all, value_all, output_all = (
         lax.all_gather(query_weight, ("row", "col"), axis=0, tiled=True),
         lax.all_gather(key_weight, ("row", "col"), axis=0, tiled=True),
-        lax.all_gather(value_weight, ("row", "col"), axis=0, tiled=True),
+        jnp.concatenate(
+            jax.lax.all_to_all(
+                jnp.stack([value_weight] * jax.lax.axis_size(("row", "col"))), ("row", "col"), 0, 0
+            ),
+            axis=0,
+        ),
         lax.all_gather(output_weight, ("row", "col"), axis=0, tiled=True),
     )
     latitudes, longitudes, features = field_rows.shape

time: 1060 us -> 883 us (0.83)
  waiting for transfers between devices: 865 us -> 671 us
  blocking collectives: 0 us -> 11.5 us
    all_gather x1 -> x0, waiting for transfers between devices: 194 us -> none  [body(): lax.all_gather(value_weight, ('row', 'col'), axis=0, tiled=True)]
    all_gather x1, waiting for transfers between devices: 194 us -> 171 us  [body(): lax.all_gather(key_weight, ('row', 'col'), axis=0, tiled=True)]
    all_to_all x1, waiting for transfers between devices: 4.25 us -> 21.8 us  [body(): jax.lax.all_to_all(jnp.stack([value_weight] * jax.lax.axis_size(('row', '...]
    all_to_all x0 -> x1, blocking collectives: none -> 11.5 us  [body(): lax.all_to_all(cotangent, 'col', split_axis=0, concat_axis=1, tiled=True)]
  transfers between devices with their start and end apart: 10 -> 9, of which waited for: 8 -> 8; matrix products, arithmetic and copies ran while one was open for 6% -> 7% of each run, Pallas kernels for 0% -> 0%
where the time goes in v1:
time: 883 us; the launch traced here: 873 us
  waiting for transfers between devices  671 us (76%)
  matrix products  72.3 us (8%)
  local copies, waits for them, and re-layouts  49.5 us (6%)
  starting transfers between devices  40.4 us (5%)
  between operations  14.8 us (2%)
  other arithmetic  13.5 us (2%)
  blocking collectives  11.5 us (1%)
    all_gather x1, waiting for transfers between devices, body(): lax.all_gather(query_weight, ('row', 'col'), axis=0, tiled=True)  194 us
    all_gather x1, waiting for transfers between devices, body(): lax.all_gather(output_weight, ('row', 'col'), axis=0, tiled=True)  191 us
    all_gather x1, waiting for transfers between devices, body(): lax.all_gather(key_weight, ('row', 'col'), axis=0, tiled=True)  171 us
    all_to_all x1, waiting for transfers between devices, body(): lax.all_to_all(spread(send_inputs), ('row', 'col'), split_axis=0, concat_...  46.8 us
    all_to_all x1, waiting for transfers between devices, body(): lax.all_to_all(returned.reshape(all_devices, CAP, features).astype(jnp.bf...  37.4 us
    dot_general x3, matrix products, contract_rows(): lax.dot_general(left, right, (((0,), (0,)), ((), ())), preferred_element_...  22.5 us
    all_to_all x1, waiting for transfers between devices, body(): jax.lax.all_to_all(jnp.stack([value_weight] * jax.lax.axis_size(('row', '...  21.8 us
    dot_general x7, matrix products, times_transposed(): lax.dot_general(left, right, (((1,), (1,)), ((), ())), preferred_element_...  21.7 us
  transfers between devices with their start and end apart: 9, of which 8 were waited for; matrix products, arithmetic and copies ran while one was open for 7% of the time, Pallas kernels for 0%

profile of v1, /device:TPU:1, one launch (start us, length us, event | category | flops | bytes accessed | tf_op | source)
XLA Modules:
  0.0 872.6 jit_solution(5125421836067008339)
XLA Ops:
  8.7 7.8 all-to-all-start.1
  17.2 6.5 all-to-all-done.1
  23.6 11.5 %all_to_all.50 = bf16[16,8,1024]{2,1,0:T(8,128)(2,1)S(1)} all-to-all(bf16[16,8,1024]{2,1,0:T(8,128)(2,1)} %param.12), channel_id=1, replica_groups=mesh['row'=8,'col'=16] {'col'}, dimensions={0} | all-to-all | bytes 524288 | tf_op jit(solution)/shard_map/all_to_all | solution.py:131
  35.1 2.3 stack.2
  37.4 8.2 all-to-all-start.2
  48.8 1.9 mul.171
  50.8 2.6 scatter_custom_fusion
  54.6 21.8 %all-to-all-done.2 = bf16[128,8,1024]{2,1,0:T(8,128)(2,1)} async-done(((bf16[128,8,1024]{2,1,0:T(8,128)(2,1)}), bf16[128,8,1024]{2,1,0:T(8,128)(2,1)}, u32[]{:S(2)}, u32[]{:S(2)}) %all-to-all-start.2) | async-done | bytes 2097184 | tf_op jit(solution)/shard_map/all_to_all | solution.py:137
  76.5 2.5 broadcast_in_dim.20
  79.0 5.8 all-to-all-start.3
  85.0 2.1 fusion.26
  87.3 171.3 %all-gather.6.cloned.1.call-done = bf16[1024,1024]{1,0:T(8,128)(2,1)} async-done(((bf16[8,1024]{1,0:T(8,128)(2,1)}), bf16[1024,1024]{1,0:T(8,128)(2,1)}) %all-gather.6.cloned.1.call-update) | async-done | bytes 2097168 | tf_op jit(solution)/shard_map/all_gather | solution.py:135
  258.6 2.1 convolution_convert_fusion.5
  260.9 193.8 %all-gather.4.cloned.1.call-done = bf16[1024,1024]{1,0:T(8,128)(2,1)} async-done(((bf16[8,1024]{1,0:T(8,128)(2,1)}), bf16[1024,1024]{1,0:T(8,128)(2,1)}) %all-gather.4.cloned.1.call-update) | async-done | bytes 2097168 | tf_op jit(solution)/shard_map/all_gather | solution.py:134
  454.7 2.1 convolution_convert_fusion.6
  456.9 1.5 fusion.75
  459.8 190.9 %all-gather.8.cloned.1.call-done = bf16[1024,1024]{1,0:T(8,128)(2,1)} async-done(((bf16[8,1024]{1,0:T(8,128)(2,1)}), bf16[1024,1024]{1,0:T(8,128)(2,1)}) %all-gather.8.cloned.1.call-update) | async-done | bytes 2097168 | tf_op jit(solution)/shard_map/all_gather | solution.py:142
  650.7 2.2 multiply_reduce_fusion.2
  654.4 2.4 scatter_custom_fusion.1
  657.9 3.7 broadcast_in_dim.23
  661.7 7.5 all-to-all-start.4
  669.2 6.2 reshape.332
  675.4 46.8 %all-to-all-done.4 = bf16[128,10,1024]{2,1,0:T(8,128)(2,1)} async-done(((bf16[128,10,1024]{2,1,0:T(8,128)(2,1)}), bf16[128,10,1024]{2,1,0:T(8,128)(2,1)}, u32[]{:S(2)}, u32[]{:S(2)}) %all-to-all-start.4) | async-done | bytes 2621472 | tf_op jit(solution)/shard_map/all_to_all | solution.py:182
  722.2 6.1 reshape.335
  728.3 5.4 fusion.6
  733.7 2.9 fusion.9
  737.4 5.9 multiply_convert_fusion.1
  743.3 2.9 fusion.4
  746.2 4.4 add_convert_fusion
  750.6 5.9 convert_element_type.202
  756.6 6.7 all-to-all-start.5
  763.3 6.9 convert_bitcast_fusion.1
  770.3 8.6 convert_bitcast_fusion
  778.9 37.4 %all-to-all-done.5 = bf16[128,10,1024]{2,1,0:T(8,128)(2,1)} async-done(((bf16[128,10,1024]{2,1,0:T(8,128)(2,1)}), bf16[128,10,1024]{2,1,0:T(8,128)(2,1)}, u32[]{:S(2)}, u32[]{:S(2)}) %all-to-all-start.5) | async-done | bytes 2621472 | tf_op jit(solution)/shard_map/all_to_all | solution.py:195
  816.3 4.7 convert_reduce_fusion
  821.0 1.9 reshape.338
  822.9 2.0 gather_fusion
  824.9 3.0 reshape.339
  827.9 2.5 reduce_sum.89
  830.6 2.5 convolution_convert_fusion.3
  834.2 2.5 convolution_convert_fusion
  837.1 2.7 convolution_convert_fusion.2
  839.9 2.8 convolution_convert_fusion.1
  842.6 2.6 fusion.77
  846.2 2.6 fusion.40
  850.0 2.1 reduce.12
  853.0 4.3 all-to-all-start.6
  857.4 6.9 convert_bitcast_fusion.2
  (105 shorter events, 18.0 us)
Async XLA Ops:
  7.2 729.5 %copy-start = (bf16[1,1024,1024]{2,1,0:T(8,128)(2,1)S(1)}, bf16[1,1024,1024]{2,1,0:T(8,128)(2,1)}, u32[]{:S(2)}) copy-start(bf16[1,1024,1024]{2,1,0:T(8,128)(2,1)} %param.21) | copy-start | bytes 6291460
  7.2 251.4 %all-gather.6.cloned.1.call-start = ((), (), s32[]{:S(2)}) async-start(), calls=%async_computation.8 | async-start | bytes 2113536 | tf_op jit(solution)/shard_map/all_gather | solution.py:135
  7.9 446.8 %all-gather.4.cloned.1.call-start = ((), (), s32[]{:S(2)}) async-start(), calls=%async_computation.7 | async-start | bytes 2113536 | tf_op jit(solution)/shard_map/all_gather | solution.py:134
  8.7 15.0 %all-to-all-start.1 = ((bf16[16,8,1024]{2,1,0:T(8,128)(2,1)}), bf16[16,8,1024]{2,1,0:T(8,128)(2,1)S(1)}, u32[]{:S(2)}, u32[]{:S(2)}) async-start(bf16[16,8,1024]{2,1,0:T(8,128)(2,1)} %param.11), calls=%async_computation.1 | async-start | bytes 524288 | tf_op jit(solution)/shard_map/all_to_all | solution.py:130
  16.4 634.3 %all-gather.8.cloned.1.call-start = ((), (), s32[]{:S(2)}) async-start(), calls=%async_computation.9 | async-start | bytes 2113536 | tf_op jit(solution)/shard_map/all_gather | solution.py:142
  35.1 12.4 %copy-start.4 = (bf16[16,8,1024]{2,1,0:T(8,128)(2,1)}, bf16[16,8,1024]{2,1,0:T(8,128)(2,1)S(1)}, u32[]{:S(2)}) copy-start(bf16[16,8,1024]{2,1,0:T(8,128)(2,1)S(1)} %all_to_all.50) | copy-start | bytes 786436
  37.4 8.2 copy-start.17
  37.4 9.7 %copy-start.18 = (f32[1,1,128,2]{2,3,1,0:T(2,128)S(1)}, f32[1,1,128,2]{2,3,1,0:T(2,128)}, u32[]{:S(2)}) copy-start(f32[1,1,128,2]{2,3,1,0:T(2,128)} %param.18) | copy-start | bytes 3076
  37.4 39.1 %all-to-all-start.2 = ((bf16[128,8,1024]{2,1,0:T(8,128)(2,1)}), bf16[128,8,1024]{2,1,0:T(8,128)(2,1)}, u32[]{:S(2)}, u32[]{:S(2)}) async-start(bf16[128,8,1024]{2,1,0:T(8,128)(2,1)} %stack.2), calls=%async_computation.2 | async-start | bytes 4194304 | tf_op jit(solution)/shard_map/all_to_all | solution.py:137
  79.0 578.9 %all-to-all-start.3 = ((bf16[128,10,1024]{2,1,0:T(8,128)(2,1)}), bf16[128,10,1024]{2,1,0:T(8,128)(2,1)}, u32[]{:S(2)}, u32[]{:S(2)}) async-start(bf16[128,10,1024]{2,1,0:T(8,128)(2,1)} %bitcast.181), calls=%async_computation.3 | async-start | bytes 8388608 | tf_op jit(solution)/shard_map/all_to_all | solution.py:185
  87.3 371.1 %copy-start.9 = (bf16[128,1024]{0,1:T(8,128)(2,1)}, bf16[128,1024]{0,1:T(8,128)(2,1)S(1)}, u32[]{:S(2)}) copy-start(bf16[128,1024]{0,1:T(8,128)(2,1)S(1)} %copy.54) | copy-start | bytes 786436
  260.9 198.9 %copy-start.11 = (bf16[128,1024]{0,1:T(8,128)(2,1)}, bf16[128,1024]{0,1:T(8,128)(2,1)S(1)}, u32[]{:S(2)}) copy-start(bf16[128,1024]{0,1:T(8,128)(2,1)S(1)} %copy.56) | copy-start | bytes 786436
  456.9 2.9 copy-start.13
  458.4 1.4 copy-start.21
  661.7 60.5 %all-to-all-start.4 = ((bf16[128,10,1024]{2,1,0:T(8,128)(2,1)}), bf16[128,10,1024]{2,1,0:T(8,128)(2,1)}, u32[]{:S(2)}, u32[]{:S(2)}) async-start(bf16[128,10,1024]{2,1,0:T(8,128)(2,1)} %bitcast.182), calls=%async_computation.4 | async-start | bytes 8388608 | tf_op jit(solution)/shard_map/all_to_all | solution.py:182
  728.3 5.4 copy-start.6
  728.3 5.4 copy-start.20
  733.7 2.9 copy-start.23
  733.7 3.6 copy-start.7
  737.4 5.9 copy-start.24
  737.4 5.9 copy-start.19
  743.3 2.9 copy-start.25
  743.3 3.0 copy-start.26
  756.6 59.7 %all-to-all-start.5 = ((bf16[128,10,1024]{2,1,0:T(8,128)(2,1)}), bf16[128,10,1024]{2,1,0:T(8,128)(2,1)}, u32[]{:S(2)}, u32[]{:S(2)}) async-start(bf16[128,10,1024]{2,1,0:T(8,128)(2,1)} %convert_element_type.202), calls=%async_computation.5 | async-start | bytes 8388608 | tf_op jit(solution)/shard_map/all_to_all | solution.py:195
  763.3 6.9 copy-start.8
  824.9 5.7 copy-start.3
  830.3 3.9 copy-start.22
  834.2 2.6 copy-start.10
  834.2 2.9 copy-start.12
  837.1 2.8 copy-start.14
  842.6 2.7 copy-start.2
  842.6 2.7 copy-start.16
  842.6 3.5 copy-start.15
  846.2 2.6 copy-start.5
  853.0 11.4 %all-to-all-start.6 = ((bf16[16,2,4096]{2,1,0:T(2,128)(2,1)}), bf16[16,2,4096]{2,1,0:T(2,128)(2,1)S(1)}, u32[]{:S(2)}, u32[]{:S(2)}) async-start(bf16[16,2,4096]{2,1,0:T(2,128)(2,1)} %reshape.379), calls=%async_computation.6 | async-start | bytes 524288 | tf_op jit(solution)/shard_map/all_to_all | solution.py:219
  857.4 8.2 copy-start.1
Sparse Core Ops, SparseCore 0:
  9.7 248.8 all-gather.5
  260.3 194.2 all-gather.3
  456.4 194.2 all-gather.7
